TPU v7x, 256 devices: a whole 4x4x8 slice. The times are simulated.
256 devices in a mesh: band: 8 (over y, core), plane: 32 (over x, z).
Axes of the slice: x: 4, y: 4, z: 8, core: 2. Of those that a mesh axis runs over, the one named last changes fastest.
Arguments:
- psi: float32 [2, 8, 4096, 128], P(None, 'band', 'plane'), may hold values from -8 to 8
- potential: float32 [96, 9216], P('plane'), may hold values from 0 to 2
- stick_column: int32 [4096], P('plane'), may hold values from 0 to 9215, as said below
- stick_length: int32 [4096], P('plane'), may hold values from 0 to 49, as said below
Outputs:
- psi_new: float32 [2, 8, 4096, 128], P(None, 'band', 'plane')
- potential_new: float32 [96, 9216], P('plane')
Inputs may be any that keep to these rules, and one draw needn't show every extreme that they name: `stick_column`: within each device's block of 128 slots the live sticks come first and the other slots are empty with column 0. Over all devices the live slots hold every column (mx mod 96) * 96 + (my mod 96) with mx * mx + my * my <= 576 exactly once, in an order drawn from the seed; some device's block is full and the others hold fewer. `stick_length`: A live slot's length is 2 h + 1, with h the largest whole number such that mx * mx + my * my + h * h <= 576 for its column; empty slots have length 0.
All inputs are finite; a program needn't handle non-finite values.
Results may differ from a plain program's by a relative error of at most 0.0001.
Values sent between devices are 32-bit elements; how exact they have to be, the bound alone decides.
No kernel may reach another device: no remote copies, remote signals or barrier semaphores. Data moves between devices by JAX's collectives and lax.ppermute only.
A program may use at most 64 MiB of HBM per device.

v0:
```python
import math

import jax
import jax.numpy as jnp
from jax import lax
from jax.sharding import PartitionSpec as P

NG = 96
RAD = 24
STICK_COEFFS = 128
BAND_DEV = 1


HIGHEST = lax.Precision.HIGHEST
TIMESTEP = 0.6
LINEAR_GAIN = 0.5
CUBIC_GAIN = 0.3


def turning(values):
    return values.astype(jnp.float32) * (2.0 * math.pi / NG)


def height_tables(lengths, columns, planes, device_list):
    order = jnp.arange(STICK_COEFFS, dtype=jnp.int32)
    height = (
        jnp.arange(device_list, dtype=jnp.int32)[None, :] * planes
        + jnp.arange(planes, dtype=jnp.int32)[:, None]
    )
    scale = NG ** (-0.5)
    wave_angle = turning(order[:, None, None] * height[None, :, :] % NG)
    wave = (jnp.cos(wave_angle) * scale, jnp.sin(wave_angle) * scale)
    half = (lengths - 1) // 2
    shift_angle = -turning(height[:, :, None] * half[None, None, :] % NG)
    shift = (jnp.cos(shift_angle), jnp.sin(shift_angle))
    mask = (order[None, :] < lengths[:, None]).astype(jnp.float32)
    first = columns // NG
    second = columns % NG
    first = jnp.where(first > NG // 2, first - NG, first)
    second = jnp.where(second > NG // 2, second - NG, second)
    depth = order[None, :] - half[:, None]
    kinetic = (
        ((first * first + second * second)[:, None] + depth * depth).astype(jnp.float32)
        / (RAD * RAD)
        * mask
    )
    return (wave, shift, mask, kinetic)


def along_height(terms, tables):
    wave, shift = (tables[0], tables[1])

    def contract(left, right):
        return jnp.einsum("bsj,jdn->bdns", left, right, precision=HIGHEST)

    upper_real = contract(terms[0], wave[0]) - contract(terms[1], wave[1])
    upper_imag = contract(terms[0], wave[1]) + contract(terms[1], wave[0])
    return jnp.stack(
        [
            upper_real * shift[0] - upper_imag * shift[1],
            upper_real * shift[1] + upper_imag * shift[0],
        ]
    )


def from_height(values, tables):
    wave, shift, mask = (tables[0], tables[1], tables[2])
    turned_real = values[0] * shift[0] + values[1] * shift[1]
    turned_imag = values[1] * shift[0] - values[0] * shift[1]

    def contract(left, right):
        return jnp.einsum("bdns,jdn->bsj", left, right, precision=HIGHEST)

    real_part = contract(turned_real, wave[0]) + contract(turned_imag, wave[1])
    imag_part = contract(turned_imag, wave[0]) - contract(turned_real, wave[1])
    return jnp.stack([real_part * mask, imag_part * mask])


def plane_tables():
    index = jnp.arange(NG, dtype=jnp.int32)
    angle = turning(index[:, None] * index[None, :] % NG)
    scale = NG ** (-0.5)
    return (jnp.cos(angle) * scale, jnp.sin(angle) * scale)


def plane_transform(values, cosine, sine):
    bands, planes = (values.shape[1], values.shape[2])
    real_part = values[0].reshape(bands, planes, NG, NG)
    imag_part = values[1].reshape(bands, planes, NG, NG)

    def inner(left, right):
        return jnp.einsum("bdmk,ky->bdmy", left, right, precision=HIGHEST)

    def outer(left, right):
        return jnp.einsum("mx,bdmy->bdxy", left, right, precision=HIGHEST)

    middle_real = inner(real_part, cosine) - inner(imag_part, sine)
    middle_imag = inner(real_part, sine) + inner(imag_part, cosine)
    final_real = outer(cosine, middle_real) - outer(sine, middle_imag)
    final_imag = outer(sine, middle_real) + outer(cosine, middle_imag)
    return jnp.stack([final_real, final_imag]).reshape(2, bands, planes, NG * NG)


def cell_slots(columns, lengths):
    count = columns.shape[0]
    target = jnp.where(lengths > 0, columns, NG * NG)
    table = jnp.full((NG * NG,), -1, jnp.int32)
    return table.at[target].set(jnp.arange(count, dtype=jnp.int32), mode="drop")


def spread_columns(values, table):
    picked = jnp.take(values, jnp.maximum(table, 0), axis=3)
    return jnp.where(table >= 0, picked, 0.0)


def modulus(field):
    return jnp.sum(field[0] * field[0] + field[1] * field[1], axis=0)


def advance(applied, power):
    factor = TIMESTEP / power
    return jnp.stack([factor * applied[1], -factor * applied[0]])


def shards(psi, potential, stick_column, stick_length):
    device_list = lax.axis_size("plane")
    planes = potential.shape[0]
    slots = stick_column.shape[0]
    bands = psi.shape[1]
    cosine, sine = plane_tables()
    own = height_tables(stick_length, stick_column, planes, device_list)
    term = psi * own[2]
    columns, lengths = (
        lax.all_gather(stick_column, "plane", axis=0, tiled=True),
        lax.all_gather(stick_length, "plane", axis=0, tiled=True),
    )
    given_cells = cell_slots(columns, lengths)
    total = term
    before = jnp.zeros((planes, NG * NG), jnp.float32)
    for power in range(1, 4):
        arrived = lax.all_to_all(
            along_height(term, own), "plane", split_axis=3, concat_axis=3, tiled=True
        ).reshape(2, bands, planes, device_list * slots)
        field = plane_transform(spread_columns(arrived, given_cells), cosine, sine)
        if power == 1:
            before = modulus(field)
        spectrum = plane_transform(field * potential, cosine, -sine)
        picked = spectrum[:, :, :, columns].reshape(2, bands, planes, device_list, slots)
        returned = lax.all_to_all(picked, "plane", split_axis=3, concat_axis=3, tiled=True)
        term = advance(from_height(returned, own) + own[3] * term, power)
        total = total + term
    arrived = lax.all_to_all(
        along_height(total, own), "plane", split_axis=3, concat_axis=3, tiled=True
    ).reshape(2, bands, planes, device_list * slots)
    after = modulus(plane_transform(spread_columns(arrived, given_cells), cosine, sine))
    change = (after - before) / BAND_DEV
    whole = lax.psum(change, "band")
    potential_new = potential + LINEAR_GAIN * whole + CUBIC_GAIN * whole * whole * whole
    return (total, potential_new)


def solution(mesh):
    in_specs = (P(None, "band", "plane", None), P("plane", None), P("plane"), P("plane"))
    out_specs = (P(None, "band", "plane", None), P("plane", None))
    return jax.shard_map(shards, mesh=mesh, in_specs=in_specs, out_specs=out_specs, check_vma=False)
```

profile of v0, /device:TPU:2, one launch (start us, length us, event | category | flops | bytes accessed | tf_op | source)
XLA Modules:
  0.0 968.3 jit_solution(16766717710354045417)
XLA Ops:
  7.8 0.7 fusion.52
  8.6 0.9 broadcast_multiply_fusion
  11.5 0.7 copy.177
  12.2 11.6 %all-to-all-start = ((f32[2,1,3,32,128]{4,0,2,1,3:T(2,128)}), f32[2,1,3,32,128]{4,0,2,1,3:T(2,128)S(1)}, u32[]{:S(2)}, u32[]{:S(2)}) async-start(f32[2,1,3,32,128]{4,0,2,1,3:T(2,128)} %copy.177), calls=%async_computation | async-start | bytes 196608 | tf_op jit(solution)/shard_map/all_to_all | solution.py:141
  23.8 39.6 %all-gather = s32[32,1,128]{2,1,0:T(1,128)S(1)} all-gather(s32[1,1,128]{2,1,0:T(1,128)} %bitcast.566), channel_id=1, replica_groups=mesh['band'=8,'plane'=32] {'plane'}, dimensions={0}, use_global_device_ids=true | all-gather | bytes 16896 | tf_op jit(solution)/shard_map/all_gather | solution.py:135
  63.4 36.7 %all-gather.1 = s32[32,1,128]{2,1,0:T(1,128)S(1)} all-gather(s32[1,1,128]{2,1,0:T(1,128)} %bitcast.567), channel_id=1, replica_groups=mesh['band'=8,'plane'=32] {'plane'}, dimensions={0}, use_global_device_ids=true | all-gather | bytes 16896 | tf_op jit(solution)/shard_map/all_gather | solution.py:134
  100.1 15.5 %scatter_custom_fusion = s32[9216]{0:T(1024)S(1)} fusion(s32[4096]{0:T(1024)S(1)} %get-tuple-element.40, s32[4096]{0:T(1024)S(1)} %iota.105, s32[]{:T(128)} %constant.56.clone.1), kind=kCustom, calls=%fused_computation.291 | custom fusion | bytes 36868 | tf_op jit(solution)/shard_map/scatter | solution.py:108
  116.4 4.3 copy.179
  120.7 65.0 %gather_fusion.3 = f32[9216,2,3]{2,1,0:T(2,128)} fusion(f32[2,3,4096]{1,0,2:T(2,128)} %bitcast.554, s32[9216]{0:T(1024)S(1)} %maximum_clamp_fusion), kind=kCustom, calls=%fused_computation.clone | custom fusion | bytes 479232 | tf_op jit(solution)/shard_map/jit(_take)/gather | solution.py:112
  185.7 42.6 %fusion.3 = f32[2,1,3,9216]{2,0,3,1:T(2,128)S(1)} fusion(f32[9216,2,3]{2,1,0:T(2,128)} %gather_fusion.3, pred[9216]{0:T(1024)(128)(4,1)S(1)} %get-tuple-element.38, pred[9216]{0:T(1024)(128)(4,1)S(1)} %get-tuple-element.37), kind=kLoop, calls=%fused_computation.15 | loop fusion | flops 110592 | bytes 460800 | tf_op jit(solution)/shard_map/jit(_where)/select_n | solution.py:113
  228.3 8.5 fusion.517
  236.8 3.1 copy.281
  240.9 3.6 copy.282
  254.3 8.9 copy.194
  263.2 31.8 %gather_fusion = f32[4096,2,3]{2,1,0:T(2,128)} fusion(f32[2,3,9216]{1,0,2:T(2,128)} %bitcast.550, s32[4096]{0:T(1024)S(1)} %get-tuple-element.39), kind=kCustom, calls=%fused_computation.4 | custom fusion | bytes 212992 | tf_op jit(solution)/shard_map/gather | solution.py:148
  295.0 5.8 copy.196
  300.9 6.5 all-to-all-start.1
  307.5 8.7 all-to-all-done.1
  316.3 0.7 convolution_bitcast_fusion.8
  317.0 0.7 convolution_bitcast_fusion.10
  317.7 0.7 fusion.26
  318.4 0.7 fusion.23
  321.1 13.5 %all_to_all.35 = f32[2,1,3,32,128]{4,0,2,1,3:T(2,128)S(1)} all-to-all(f32[2,1,3,32,128]{4,0,2,1,3:T(2,128)S(1)} %copy.199), channel_id=1, replica_groups=mesh['band'=8,'plane'=32] {'plane'}, dimensions={3} | all-to-all | bytes 196608 | tf_op jit(solution)/shard_map/all_to_all | solution.py:141
  334.6 4.3 copy.201
  339.0 65.0 %gather_fusion.4 = f32[9216,2,3]{2,1,0:T(2,128)} fusion(f32[2,3,4096]{1,0,2:T(2,128)} %bitcast.555, s32[9216]{0:T(1024)S(1)} %maximum_clamp_fusion), kind=kCustom, calls=%fused_computation.1.clone | custom fusion | bytes 479232 | tf_op jit(solution)/shard_map/jit(_take)/gather | solution.py:112
  403.9 42.6 %fusion.2 = f32[2,1,3,9216]{2,0,3,1:T(2,128)S(1)} fusion(f32[9216,2,3]{2,1,0:T(2,128)} %gather_fusion.4, pred[9216]{0:T(1024)(128)(4,1)S(1)} %get-tuple-element.38, pred[9216]{0:T(1024)(128)(4,1)S(1)} %get-tuple-element.37), kind=kLoop, calls=%fused_computation.13 | loop fusion | flops 110592 | bytes 460800 | tf_op jit(solution)/shard_map/jit(_where)/select_n | solution.py:113
  446.5 8.5 fusion.516
  455.0 3.1 copy.285
  459.1 3.3 copy.286
  472.2 8.9 copy.216
  481.1 31.8 %gather_fusion.1 = f32[4096,2,3]{2,1,0:T(2,128)} fusion(f32[2,3,9216]{1,0,2:T(2,128)} %bitcast.552, s32[4096]{0:T(1024)S(1)} %get-tuple-element.39), kind=kCustom, calls=%fused_computation.5 | custom fusion | bytes 212992 | tf_op jit(solution)/shard_map/gather | solution.py:148
  513.0 5.8 copy.218
  518.8 5.5 all-to-all-start.3
  524.3 8.9 all-to-all-done.3
  533.3 0.7 convolution_bitcast_fusion.4
  534.0 0.7 convolution_bitcast_fusion.6
  534.7 0.7 fusion.32
  535.4 0.7 fusion.29
  538.1 13.5 %all_to_all.36 = f32[2,1,3,32,128]{4,0,2,1,3:T(2,128)S(1)} all-to-all(f32[2,1,3,32,128]{4,0,2,1,3:T(2,128)S(1)} %copy.221), channel_id=1, replica_groups=mesh['band'=8,'plane'=32] {'plane'}, dimensions={3} | all-to-all | bytes 196608 | tf_op jit(solution)/shard_map/all_to_all | solution.py:141
  551.6 4.3 copy.223
  556.0 65.0 %gather_fusion.5 = f32[9216,2,3]{2,1,0:T(2,128)} fusion(f32[2,3,4096]{1,0,2:T(2,128)} %bitcast.556, s32[9216]{0:T(1024)S(1)} %maximum_clamp_fusion), kind=kCustom, calls=%fused_computation.2.clone | custom fusion | bytes 479232 | tf_op jit(solution)/shard_map/jit(_take)/gather | solution.py:112
  620.9 42.6 %fusion.1 = f32[2,1,3,9216]{2,0,3,1:T(2,128)S(1)} fusion(f32[9216,2,3]{2,1,0:T(2,128)} %gather_fusion.5, pred[9216]{0:T(1024)(128)(4,1)S(1)} %get-tuple-element.38, pred[9216]{0:T(1024)(128)(4,1)S(1)} %get-tuple-element.37), kind=kLoop, calls=%fused_computation.11 | loop fusion | flops 110592 | bytes 460800 | tf_op jit(solution)/shard_map/jit(_where)/select_n | solution.py:113
  663.5 8.5 fusion.515
  672.0 3.1 copy.289
  676.1 3.3 copy.290
  689.2 8.9 copy.238
  698.1 31.8 %gather_fusion.2 = f32[4096,2,3]{2,1,0:T(2,128)} fusion(f32[2,3,9216]{1,0,2:T(2,128)} %bitcast.551, s32[4096]{0:T(1024)S(1)} %get-tuple-element.39), kind=kCustom, calls=%fused_computation.6 | custom fusion | bytes 212992 | tf_op jit(solution)/shard_map/gather | solution.py:148
  729.9 5.8 copy.240
  735.7 5.0 all-to-all-start.5
  741.0 8.8 all-to-all-done.5
  749.9 0.7 convolution_bitcast_fusion
  750.5 0.7 convolution_bitcast_fusion.2
  751.2 0.7 fusion.38
  751.9 0.7 fusion.35
  754.8 13.5 %all_to_all.37 = f32[2,1,3,32,128]{4,0,2,1,3:T(2,128)S(1)} all-to-all(f32[2,1,3,32,128]{4,0,2,1,3:T(2,128)S(1)} %copy.243), channel_id=1, replica_groups=mesh['band'=8,'plane'=32] {'plane'}, dimensions={3} | all-to-all | bytes 196608 | tf_op jit(solution)/shard_map/all_to_all | solution.py:152
  768.3 4.3 copy.245
  772.6 65.0 %gather_fusion.6 = f32[9216,2,3]{2,1,0:T(2,128)} fusion(f32[2,3,4096]{1,0,2:T(2,128)} %bitcast.553, s32[9216]{0:T(1024)S(1)} %maximum_clamp_fusion), kind=kCustom, calls=%fused_computation.3.clone | custom fusion | bytes 479232 | tf_op jit(solution)/shard_map/jit(_take)/gather | solution.py:112
  837.6 42.6 %fusion = f32[2,1,3,9216]{2,0,3,1:T(2,128)S(1)} fusion(f32[9216,2,3]{2,1,0:T(2,128)} %gather_fusion.6, pred[9216]{0:T(1024)(128)(4,1)S(1)} %get-tuple-element.38, pred[9216]{0:T(1024)(128)(4,1)S(1)} %get-tuple-element.37), kind=kLoop, calls=%fused_computation.9 | loop fusion | flops 110592 | bytes 460800 | tf_op jit(solution)/shard_map/jit(_where)/select_n | solution.py:113
  880.1 8.5 fusion.514
  888.6 3.1 copy.293
  892.7 3.1 copy.294
  899.1 0.8 sub.241
  899.9 59.6 %all-reduce.2.cloned.1.call-done = f32[3,9216]{1,0:T(4,128)} async-done(((f32[3,9216]{1,0:T(4,128)}), f32[3,9216]{1,0:T(4,128)}) %all-reduce.2.cloned.1.call-update) | async-done | bytes 110608 | tf_op jit(solution)/shard_map/psum | solution.py:157
  959.6 1.6 fusion.39
  (153 shorter events, 46.0 us)
Async XLA Ops:
  12.2 104.2 %all-to-all-start = ((f32[2,1,3,32,128]{4,0,2,1,3:T(2,128)}), f32[2,1,3,32,128]{4,0,2,1,3:T(2,128)S(1)}, u32[]{:S(2)}, u32[]{:S(2)}) async-start(f32[2,1,3,32,128]{4,0,2,1,3:T(2,128)} %copy.177), calls=%async_computation | async-start | bytes 196608 | tf_op jit(solution)/shard_map/all_to_all | solution.py:141
  236.8 11.4 %copy-start = (f32[3,9216]{1,0:T(4,128)S(1)}, f32[3,9216]{1,0:T(4,128)}, u32[]{:S(2)}) copy-start(f32[3,9216]{1,0:T(4,128)} %param.7) | copy-start | bytes 331780
  249.7 57.6 %copy-start.3 = (s32[128]{0:T(128)S(1)}, s32[128]{0:T(128)}, u32[]{:S(2)}) copy-start(s32[128]{0:T(128)} %param.9) | copy-start | bytes 1540
  252.4 66.7 %copy-start.1 = (f32[2,1,128,128]{3,2,1,0:T(8,128)S(1)}, f32[2,1,128,128]{3,2,1,0:T(8,128)}, u32[]{:S(2)}) copy-start(f32[2,1,128,128]{3,2,1,0:T(8,128)} %param.6) | copy-start | bytes 393220
  300.9 15.4 %all-to-all-start.1 = ((f32[2,1,3,32,128]{4,0,2,1,3:T(2,128)}), f32[2,1,3,32,128]{4,0,2,1,3:T(2,128)S(1)}, u32[]{:S(2)}, u32[]{:S(2)}) async-start(f32[2,1,3,32,128]{4,0,2,1,3:T(2,128)} %copy.196), calls=%async_computation.1 | async-start | bytes 196608 | tf_op jit(solution)/shard_map/all_to_all | solution.py:149
  518.8 14.4 %all-to-all-start.3 = ((f32[2,1,3,32,128]{4,0,2,1,3:T(2,128)}), f32[2,1,3,32,128]{4,0,2,1,3:T(2,128)S(1)}, u32[]{:S(2)}, u32[]{:S(2)}) async-start(f32[2,1,3,32,128]{4,0,2,1,3:T(2,128)} %copy.218), calls=%async_computation.3 | async-start | bytes 196608 | tf_op jit(solution)/shard_map/all_to_all | solution.py:149
  735.7 14.0 %all-to-all-start.5 = ((f32[2,1,3,32,128]{4,0,2,1,3:T(2,128)}), f32[2,1,3,32,128]{4,0,2,1,3:T(2,128)S(1)}, u32[]{:S(2)}, u32[]{:S(2)}) async-start(f32[2,1,3,32,128]{4,0,2,1,3:T(2,128)} %copy.240), calls=%async_computation.5 | async-start | bytes 196608 | tf_op jit(solution)/shard_map/all_to_all | solution.py:149
  740.7 218.9 %all-reduce.2.cloned.1.call-start = ((), (), s32[]{:S(2)}) async-start(), calls=%async_computation.7 | async-start | bytes 294912 | tf_op jit(solution)/shard_map/psum | solution.py:157
  752.7 127.4 %copy-start.2 = (f32[2,1,128,128]{3,2,1,0:T(8,128)}, f32[2,1,128,128]{3,2,1,0:T(8,128)S(1)}, u32[]{:S(2)}) copy-start(f32[2,1,128,128]{3,2,1,0:T(8,128)S(1)} %maximum_add_fusion.3) | copy-start | bytes 393220
Sparse Core Ops, SparseCore 0:
  900.0 59.4 all-reduce.1
where the time goes:
time: 975 us; the launch traced here: 968 us
  local copies, waits for them, and re-layouts  501 us (51%)
  other arithmetic  177 us (18%)
  blocking collectives  117 us (12%)
  waiting for transfers between devices  86.1 us (9%)
  matrix products  43.7 us (4%)
  starting transfers between devices  28.8 us (3%)
  between operations  15.4 us (2%)
    gather x4, local copies, waits for them, and re-layouts, spread_columns(): picked = jnp.take(values, jnp.maximum(table, 0), axis=3)  260 us
    select_n x4, other arithmetic, spread_columns(): return jnp.where(table >= 0, picked, 0.0)  170 us
    gather x3, local copies, waits for them, and re-layouts, shards(): spectrum[:, :, :, columns].reshape(2, bands, planes, device_list, slots)  95.5 us
    psum x1, waiting for transfers between devices, shards(): whole = lax.psum(change, 'band')  59.6 us
    all_gather x1, blocking collectives, shards(): lax.all_gather(stick_length, 'plane', axis=0, tiled=True)  39.6 us
    all_gather x1, blocking collectives, shards(): lax.all_gather(stick_column, 'plane', axis=0, tiled=True)  36.7 us
    slice x7, local copies, waits for them, and re-layouts, plane_transform(): imag_part = values[1].reshape(bands, planes, NG, NG)  35.9 us
    another operation x15, local copies, waits for them, and re-layouts, plane_transform(): jnp.stack([final_real, final_imag]).reshape(2, bands, planes, NG * NG)  29.1 us
  transfers between devices with their start and end apart: 5, of which 4 were waited for; matrix products, arithmetic and copies ran while one was open for 2% of the time, Pallas kernels for 0%

commit v1 on v0

v1 whole, which is shorter than its diff:
```python
import functools
import math

import jax
import jax.numpy as jnp
import ml_dtypes
import numpy as np
from jax import lax
from jax.experimental import pallas as pl
from jax.experimental.pallas import tpu as pltpu
from jax.sharding import Mesh
from jax.sharding import PartitionSpec as P

NG = 96
RAD = 24
HALF = 64
LANES = 128
PLANES = 3
OWNERS = 32
SLOTS = 128
TIMESTEP = 0.6
LINEAR_GAIN = 0.5
CUBIC_GAIN = 0.3

F32 = jnp.float32
BF16 = jnp.bfloat16
NT = (((1,), (1,)), ((), ()))


def halves(values):
    high = values.astype(ml_dtypes.bfloat16)
    low = (values - high.astype(np.float64)).astype(ml_dtypes.bfloat16)
    return high, low


def wave(count, order):
    turns = np.outer(np.arange(count), np.arange(order) - RAD) % NG
    angle = turns * (2.0 * math.pi / NG)
    scale = NG**-0.5
    return np.cos(angle) * scale, np.sin(angle) * scale


def height_table():
    cosine, sine = wave(NG, 2 * RAD + 1)
    table = np.zeros((OWNERS, 8, LANES))
    order = 2 * RAD + 1
    for owner in range(OWNERS):
        for plane in range(PLANES):
            z = PLANES * owner + plane
            table[owner, 2 * plane, :order] = cosine[z]
            table[owner, 2 * plane, HALF : HALF + order] = -sine[z]
            table[owner, 2 * plane + 1, :order] = sine[z]
            table[owner, 2 * plane + 1, HALF : HALF + order] = cosine[z]
    return table.reshape(OWNERS * 8, LANES)


def second_table():
    cosine, sine = wave(NG, 2 * RAD + 1)
    order = 2 * RAD + 1
    table = np.zeros((LANES, 2 * LANES))
    table[:order, :NG] = cosine.T
    table[HALF : HALF + order, :NG] = -sine.T
    table[:order, LANES : LANES + NG] = sine.T
    table[HALF : HALF + order, LANES : LANES + NG] = cosine.T
    return table


def first_table():
    cosine, sine = wave(NG, 2 * RAD + 1)
    table = np.zeros((2 * NG, HALF))
    table[:NG, : 2 * RAD + 1] = cosine
    table[NG:, : 2 * RAD + 1] = sine
    return table


def tables():
    high, low = halves(height_table())
    second_high, second_low = halves(second_table())
    first_high, first_low = halves(first_table())
    back = np.concatenate([first_table()[:NG].T, first_table()[NG:].T], axis=0)
    back_high, back_low = halves(back)
    stick = (
        np.concatenate([high, high], axis=1),
        low,
        high,
    )
    plane = (
        np.concatenate([second_high, second_high], axis=0),
        second_low,
        np.concatenate([first_high, first_low, first_high], axis=1),
        np.concatenate([back_high, back_low, back_high], axis=1),
        np.ascontiguousarray(second_high.T),
        np.ascontiguousarray(second_low.T),
    )
    return stick, plane


def split(values):
    high = values.astype(BF16)
    return high, (values - high.astype(F32)).astype(BF16)


def dot(left, right):
    return jnp.dot(left, right, preferred_element_type=F32)


def lanes_of(shape):
    return lax.broadcasted_iota(jnp.int32, shape, 1)


def stick_codes(column, length):
    first = jnp.floor((column + 0.5) * (1.0 / NG))
    second = column - NG * first
    first = jnp.where(first > NG // 2, first - NG, first)
    second = jnp.where(second > NG // 2, second - NG, second)
    live = length > 0.0
    return jnp.where(live, first + RAD, -1.0), jnp.where(live, second + RAD, -1.0)


def along_slots(row):
    return jnp.broadcast_to(row, (SLOTS, LANES)).T


def shift_lanes(values, amount, direction):
    for bit in range(5):
        step = 1 << bit
        moved = pltpu.roll(values, step if direction > 0 else LANES - step, 1)
        values = jnp.where((amount & step) != 0, moved, values)
    return values


def lane_shift(length_row):
    length = along_slots(length_row).astype(jnp.int32)
    return jnp.clip(RAD - ((length - 1) >> 1), 0, RAD), length


def send_heights(term, codes, stick_pair, stick_low, out_ref):
    high, low = split(term)
    both = jnp.concatenate([high, low], axis=1)
    rows = lax.dot_general(stick_pair, both, NT, preferred_element_type=F32)
    rows = rows + lax.dot_general(stick_low, high, NT, preferred_element_type=F32)
    rows = rows.reshape(OWNERS, 8, SLOTS)
    place = lax.broadcasted_iota(jnp.int32, (OWNERS, 8, SLOTS), 1)
    rows = jnp.where(place == 6, codes[0][None], rows)
    out_ref[...] = jnp.where(place == 7, codes[1][None], rows)


def start_kernel(psi_ref, column_ref, length_ref, pair_ref, low_ref, term_ref, kinetic_ref, out_ref):
    column, length_row = column_ref[...], length_ref[...]
    codes = stick_codes(column, length_row)
    amount, length = lane_shift(length_row)
    lane = lanes_of((SLOTS, LANES))
    inside = lane < length
    real_part = shift_lanes(jnp.where(inside, psi_ref[0], 0.0), amount, 1)
    imag_part = shift_lanes(jnp.where(inside, psi_ref[1], 0.0), amount, 1)
    term = real_part + pltpu.roll(imag_part, HALF, 1)
    term_ref[...] = term
    depth = (lane & (HALF - 1)) - RAD
    first = along_slots(codes[0]) - RAD
    second = along_slots(codes[1]) - RAD
    spread = depth.astype(F32)
    kinetic = (first * first + second * second + spread * spread) / (RAD * RAD)
    valid = (jnp.abs(depth) <= ((length - 1) >> 1)) & (length > 0)
    kinetic_ref[...] = jnp.where(valid, kinetic, -1.0)
    send_heights(term, codes, pair_ref[...], low_ref[...], out_ref)


def stick_kernel(power, last, *refs):
    if last:
        (got_ref, term_ref, total_ref, kinetic_ref, column_ref, length_ref, pair_ref, low_ref, high_ref,
         psi_ref, out_ref) = refs
    else:
        (got_ref, term_ref, total_ref, kinetic_ref, column_ref, length_ref, pair_ref, low_ref, high_ref,
         next_ref, sum_ref, out_ref) = refs
    codes = stick_codes(column_ref[...], length_ref[...])
    got = got_ref[...].reshape(OWNERS * 8, SLOTS).T
    high, low = split(got)
    back_high, back_low = high_ref[...], low_ref[...]
    applied = dot(high, back_high) + dot(low, back_high) + dot(high, back_low)
    kinetic = kinetic_ref[...]
    applied = jnp.where(kinetic >= 0.0, applied + kinetic * term_ref[...], 0.0)
    factor = TIMESTEP / power
    lane = lanes_of((SLOTS, LANES))
    term = pltpu.roll(applied, HALF, 1) * jnp.where(lane < HALF, factor, -factor)
    total = total_ref[...] + term
    if last:
        amount, _ = lane_shift(length_ref[...])
        lower = lane < HALF
        psi_ref[0] = shift_lanes(jnp.where(lower, total, 0.0), amount, -1)
        psi_ref[1] = shift_lanes(jnp.where(lower, pltpu.roll(total, HALF, 1), 0.0), amount, -1)
        send_heights(total, codes, pair_ref[...], low_ref[...], out_ref)
    else:
        next_ref[...] = term
        sum_ref[...] = total
        send_heights(term, codes, pair_ref[...], low_ref[...], out_ref)


def plane_kernel(stage, *refs):
    refs = list(refs)
    got_ref = refs.pop(0)
    other_ref = refs.pop(0)
    second_pair, second_low, first_all, back_all, inner_high, inner_low = refs[:6]
    refs = refs[6:]
    spread_ref, cell_ref = refs[-2:]
    outs = refs[:-2]
    row = lax.broadcasted_iota(jnp.int32, (HALF, SLOTS), 0).astype(F32)

    def place(owner, carry):
        got = got_ref[owner]
        high = got.astype(BF16).astype(F32)
        low = got - high
        at = pl.ds(pl.multiple_of(owner * SLOTS, SLOTS), SLOTS)
        mine = row == got[6:7]
        for r in range(2 * PLANES):
            spread_ref[r * HALF : (r + 1) * HALF, at] = jnp.where(mine, high[r : r + 1], 0.0).astype(BF16)
            spread_ref[(r + 6) * HALF : (r + 7) * HALF, at] = jnp.where(mine, low[r : r + 1], 0.0).astype(BF16)
        cell = jnp.where(row == got[7:8], 1.0, 0.0).astype(BF16)
        cell_ref[:HALF, at] = cell
        cell_ref[HALF:, at] = cell
        return carry

    lax.fori_loop(0, OWNERS, place, 0, unroll=4)
    grid = lax.dot_general(spread_ref[...], cell_ref[:HALF], NT, preferred_element_type=F32)
    grid = (grid[: 6 * HALF] + grid[6 * HALF :]).reshape(PLANES, 2, HALF, HALF)
    lined = jnp.concatenate([grid[:, 0], grid[:, 1]], axis=2).reshape(PLANES * HALF, LANES)
    high, low = split(lined)
    middle = dot(jnp.concatenate([high, low], axis=1), second_pair[...]) + dot(high, second_low[...])
    returned = []
    for plane in range(PLANES):
        high, low = split(middle[plane * HALF : (plane + 1) * HALF])
        both = dot(first_all[...], jnp.concatenate([high, high, low], axis=0))
        real_part = both[:NG, :LANES] - both[NG:, LANES:]
        imag_part = both[NG:, :LANES] + both[:NG, LANES:]
        if stage == "first":
            outs[1][plane] = real_part * real_part + imag_part * imag_part
        if stage == "last":
            outs[0][plane] = real_part * real_part + imag_part * imag_part - other_ref[plane]
            continue
        weight = other_ref[plane]
        field = jnp.concatenate([real_part * weight, imag_part * weight], axis=1)
        high, low = split(field)
        both = dot(back_all[...], jnp.concatenate([high, high, low], axis=0))
        returned.append(
            jnp.concatenate(
                [both[:HALF, :LANES] + both[HALF:, LANES:], both[:HALF, LANES:] - both[HALF:, :LANES]],
                axis=1,
            )
        )
    if stage == "last":
        return
    high, low = split(jnp.concatenate(returned, axis=0))
    rows = dot(high, inner_high[...]) + dot(low, inner_high[...]) + dot(high, inner_low[...])
    rows = rows.reshape(PLANES, 1, HALF, LANES)
    rows = jnp.concatenate([rows[..., :HALF], rows[..., HALF:]], axis=1).reshape(6 * HALF, HALF)
    high, low = split(rows)
    both = jnp.concatenate([high, low], axis=1)
    tail = jnp.zeros((2, SLOTS), F32)

    def pick(pair, carry):
        at = pl.ds(pl.multiple_of(pair * 2 * SLOTS, 2 * SLOTS), 2 * SLOTS)
        found = dot(both, cell_ref[:, at]).reshape(6, HALF, 2 * SLOTS)
        for side in range(2):
            mine = row == got_ref[2 * pair + side][6:7]
            chosen = jnp.where(mine[None], found[:, :, side * SLOTS : (side + 1) * SLOTS], 0.0)
            outs[0][2 * pair + side] = jnp.concatenate([jnp.sum(chosen, axis=1), tail], axis=0)
        return carry

    lax.fori_loop(0, OWNERS // 2, pick, 0, unroll=4)


def call(kernel, name, shapes, scratch=()):
    return pl.pallas_call(
        kernel,
        out_shape=tuple(jax.ShapeDtypeStruct(s, F32) for s in shapes),
        scratch_shapes=scratch,
        name=name,
        compiler_params=pltpu.CompilerParams(vmem_limit_bytes=48 << 20),
    )


def plane_call(stage, got, other, plane_tables):
    wire = (OWNERS, 8, SLOTS)
    cells = (PLANES, NG, LANES)
    shapes = {"first": (wire, cells), "next": (wire,), "last": (cells,)}[stage]
    scratch = [pltpu.VMEM((12 * HALF, OWNERS * SLOTS), BF16), pltpu.VMEM((2 * HALF, OWNERS * SLOTS), BF16)]
    return call(functools.partial(plane_kernel, stage), "plane_" + stage, shapes, scratch)(got, other, *plane_tables)


def exchange(rows):
    return lax.all_to_all(rows, ("x", "z"), split_axis=0, concat_axis=0, tiled=True)


def swap(values, axis, mask):
    size = lax.axis_size(axis)
    return lax.ppermute(values, axis, [(s, s ^ mask) for s in range(size)])


def shards(psi, potential, stick_column, stick_length):
    stick_np, plane_np = tables()
    stick_tables = tuple(map(jnp.asarray, stick_np))
    plane_tables = tuple(map(jnp.asarray, plane_np))
    wire, state = (OWNERS, 8, SLOTS), (SLOTS, LANES)
    column = stick_column.astype(F32).reshape(1, SLOTS)
    length = stick_length.astype(F32).reshape(1, SLOTS)
    weight = jnp.pad(potential.reshape(PLANES, NG, NG), ((0, 0), (0, 0), (0, LANES - NG)))
    term, kinetic, rows = call(start_kernel, "start", (state, state, wire))(
        psi.reshape(2, SLOTS, LANES), column, length, *stick_tables[:2]
    )
    total = term
    before = None
    psi_new = None
    for power in range(1, 4):
        got = exchange(rows)
        if power == 1:
            rows, before = plane_call("first", got, weight, plane_tables)
        else:
            (rows,) = plane_call("next", got, weight, plane_tables)
        got = exchange(rows)
        last = power == 3
        shapes = ((2, SLOTS, LANES), wire) if last else (state, state, wire)
        given = call(functools.partial(stick_kernel, power, last), f"stick_{power}", shapes)(
            got, term, total, kinetic, column, length, *stick_tables
        )
        if last:
            psi_new, rows = given
        else:
            term, total, rows = given
    (change,) = plane_call("last", exchange(rows), before, plane_tables)
    change = change + swap(change, "core", 1)
    change = change + swap(change, "y", 1)
    change = change + swap(change, "y", 2)
    added = weight + LINEAR_GAIN * change + CUBIC_GAIN * change * change * change
    potential_new = added[:, :, :NG].reshape(PLANES, NG * NG)
    return psi_new.reshape(2, 1, SLOTS, LANES), potential_new


def solution(mesh):
    fine = Mesh(mesh.devices.reshape(4, 2, 4, 8), ("y", "core", "x", "z"))
    band, plane = ("y", "core"), ("x", "z")
    in_specs = (P(None, band, plane, None), P(plane, None), P(plane), P(plane))
    out_specs = (P(None, band, plane, None), P(plane, None))
    return jax.shard_map(shards, mesh=fine, in_specs=in_specs, out_specs=out_specs, check_vma=False)
```

time: 975 us -> 156 us (0.16)
  local copies, waits for them, and re-layouts: 501 us -> 3.69 us
  other arithmetic: 177 us -> 0.75 us
  waiting for transfers between devices: 86.1 us -> 18 us
  matrix products: 43.7 us -> 0 us
  blocking collectives: 117 us -> 83.3 us
  Pallas kernels: 0 us -> 31.6 us
  between operations: 15.4 us -> 0.84 us
  starting transfers between devices: 28.8 us -> 16.8 us
    gather x7 -> x0, local copies, waits for them, and re-layouts: 355 us -> none  [the longest x4 260 us: spread_columns(): picked = jnp.take(values, jnp.maximum(table, 0), axis=3)]
    select_n x5 -> x0, other arithmetic: 171 us -> none  [the longest x4 170 us: spread_columns(): return jnp.where(table >= 0, picked, 0.0)]
    all_gather x2 -> x0, blocking collectives: 76.3 us -> none  [the longest x1 39.6 us: shards(): lax.all_gather(stick_length, 'plane', axis=0, tiled=True)]
    psum x1 -> x0, waiting for transfers between devices: 59.6 us -> none  [shards(): whole = lax.psum(change, 'band')]
    another operation x33 -> x0, local copies, waits for them, and re-layouts: 56.7 us -> none  [the longest x15 29.1 us: plane_transform(): jnp.stack([final_real, final_imag]).reshape(2, bands, planes, NG * NG)]
    dot_general x84 -> x0, matrix products: 43.7 us -> none  [the longest x28 14.6 us: outer(): return jnp.einsum('mx,bdmy->bdxy', left, right, precision=HIGHEST)]
    all_to_all x3 -> x6, blocking collectives: 40.5 us -> 83.3 us  [exchange(): lax.all_to_all(rows, ('x', 'z'), split_axis=0, concat_axis=0, tiled=True)]
    slice x10 -> x0, local copies, waits for them, and re-layouts: 36.1 us -> none  [the longest x7 35.9 us: plane_transform(): imag_part = values[1].reshape(bands, planes, NG, NG)]
  transfers between devices with their start and end apart: 5 -> 4, of which waited for: 4 -> 4; matrix products, arithmetic and copies ran while one was open for 2% -> 0% of each run, Pallas kernels for 0% -> 0%
where the time goes in v1:
time: 156 us; the launch traced here: 155 us
  blocking collectives  83.3 us (53%)
  Pallas kernels  31.6 us (20%)
  waiting for transfers between devices  18 us (12%)
  starting transfers between devices  16.8 us (11%)
  local copies, waits for them, and re-layouts  3.69 us (2%)
    all_to_all x6, blocking collectives, exchange(): lax.all_to_all(rows, ('x', 'z'), split_axis=0, concat_axis=0, tiled=True)  83.3 us
    pallas_call x4, Pallas kernels, plane_call(): call(functools.partial(plane_kernel, stage), 'plane_' + stage, shapes, sc...  27.7 us
    all_to_all x1, starting transfers between devices, exchange(): lax.all_to_all(rows, ('x', 'z'), split_axis=0, concat_axis=0, tiled=True)  11.7 us
    ppermute x3, waiting for transfers between devices, swap(): return lax.ppermute(values, axis, [(s, s ^ mask) for s in range(size)])  9.14 us
    all_to_all x1, waiting for transfers between devices, exchange(): lax.all_to_all(rows, ('x', 'z'), split_axis=0, concat_axis=0, tiled=True)  8.85 us
    ppermute x3, starting transfers between devices, swap(): return lax.ppermute(values, axis, [(s, s ^ mask) for s in range(size)])  5.03 us
  transfers between devices with their start and end apart: 4, of which 4 were waited for; matrix products, arithmetic and copies ran while one was open for 0% of the time, Pallas kernels for 0%

profile of v1, /device:TPU:2, one launch (start us, length us, event | category | flops | bytes accessed | tf_op | source)
XLA Modules:
  0.0 154.9 jit_solution(12289082537196692128)
XLA Ops:
  0.6 0.7 convert_bitcast_fusion
  1.3 0.0 copy-start.1
  1.3 0.9 copy-done.1
  2.2 0.0 copy-start.8
  2.2 0.8 copy-done.8
  3.0 0.0 copy-start.11
  3.1 0.9 copy-done.11
  4.0 1.4 start.1
  5.3 0.0 copy-start.12
  5.3 11.7 %all-to-all-start = ((f32[32,8,128]{2,1,0:T(8,128)}), f32[32,8,128]{2,1,0:T(8,128)S(1)}, u32[]{:S(2)}, u32[]{:S(2)}) async-start(f32[32,8,128]{2,1,0:T(8,128)} %get-tuple-element.15), calls=%async_computation | async-start | bytes 262144 | tf_op jit(solution)/shard_map/all_to_all | solution.py:290
  17.1 0.0 copy-done.12
  17.1 0.0 copy-start.4
  17.1 0.0 copy-start.6
  17.1 0.0 copy-start.7
  17.1 0.1 reshape.25
  17.3 0.0 copy-start
  17.3 0.0 copy-start.3
  17.3 0.0 copy-start.5
  17.3 8.8 %all-to-all-done.refs_0_ = f32[32,8,128]{2,1,0:T(8,128)S(1)} async-done(((f32[32,8,128]{2,1,0:T(8,128)}), f32[32,8,128]{2,1,0:T(8,128)S(1)}, u32[]{:S(2)}, u32[]{:S(2)}) %all-to-all-start) | async-done | bytes 131104 | tf_op jit(solution)/shard_map/all_to_all | solution.py:290
  26.2 0.0 copy-done.4
  26.2 0.0 copy-done.6
  26.2 0.0 copy-done.7
  26.2 0.0 copy-done
  26.2 0.0 copy-done.3
  26.2 0.0 copy-done.5
  26.2 7.6 %plane_first.1 = (f32[32,8,128]{2,1,0:T(8,128)S(1)}, f32[3,96,128]{2,1,0:T(8,128)S(1)}) custom-call(f32[32,8,128]{2,1,0:T(8,128)S(1)} %all-to-all-done.refs_0_, f32[3,96,128]{2,1,0:T(8,128)S(1)} %pad.4.refs_1_, bf16[256,256]{1,0:T(8,128)(2,1)S(1)} %copy-done, bf16[128,256]{1,0:T(8,128)(2,1)S(1)} %copy-done.7, bf16[192,192]{1,0:T(8,128)(2,1)S(1)} %copy-done.4, ...), custom_call_target="tpu_custom_call" | custom-call | tf_op jit(solution)/shard_map/plane_first/pallas_call | solution.py:286
  33.8 0.0 copy-start.2
  33.8 0.0 copy-start.9
  33.8 0.0 copy-start.10
  33.9 14.1 %all_to_all.35.refs_0_ = f32[32,8,128]{2,1,0:T(8,128)S(1)} all-to-all(f32[32,8,128]{2,1,0:T(8,128)S(1)} %get-tuple-element.16), channel_id=1, replica_groups=mesh['y'=4,'core'=2,'x'=4,'z'=8] {'x','z'}, dimensions={0} | all-to-all | bytes 262144 | tf_op jit(solution)/shard_map/all_to_all | solution.py:290
  47.9 0.0 copy-done.2
  47.9 0.0 copy-done.9
  47.9 0.0 copy-done.10
  47.9 0.5 stick_1.1
  48.5 13.9 %all_to_all.36.refs_0_ = f32[32,8,128]{2,1,0:T(8,128)S(1)} all-to-all(f32[32,8,128]{2,1,0:T(8,128)S(1)} %get-tuple-element.19), channel_id=1, replica_groups=mesh['y'=4,'core'=2,'x'=4,'z'=8] {'x','z'}, dimensions={0} | all-to-all | bytes 262144 | tf_op jit(solution)/shard_map/all_to_all | solution.py:290
  62.4 7.6 %plane_next.2 = f32[32,8,128]{2,1,0:T(8,128)S(1)} custom-call(f32[32,8,128]{2,1,0:T(8,128)S(1)} %all_to_all.36.refs_0_, f32[3,96,128]{2,1,0:T(8,128)S(1)} %pad.4.refs_1_, bf16[256,256]{1,0:T(8,128)(2,1)S(1)} %copy-done, bf16[128,256]{1,0:T(8,128)(2,1)S(1)} %copy-done.7, bf16[192,192]{1,0:T(8,128)(2,1)S(1)} %copy-done.4, bf16[128,288]{1,0:T(8,128)(2,1)S(1)} %copy-done.3, ...), custom_call_target="tpu_custom_call" | custom-call | tf_op jit(solution)/shard_map/plane_next/pallas_call | solution.py:286
  69.9 13.8 %all_to_all.37.refs_0_ = f32[32,8,128]{2,1,0:T(8,128)S(1)} all-to-all(f32[32,8,128]{2,1,0:T(8,128)S(1)} %plane_next.2), channel_id=1, replica_groups=mesh['y'=4,'core'=2,'x'=4,'z'=8] {'x','z'}, dimensions={0} | all-to-all | bytes 262144 | tf_op jit(solution)/shard_map/all_to_all | solution.py:290
  83.7 0.5 stick_2.1
  84.3 13.9 %all_to_all.38.refs_0_ = f32[32,8,128]{2,1,0:T(8,128)S(1)} all-to-all(f32[32,8,128]{2,1,0:T(8,128)S(1)} %get-tuple-element.22), channel_id=1, replica_groups=mesh['y'=4,'core'=2,'x'=4,'z'=8] {'x','z'}, dimensions={0} | all-to-all | bytes 262144 | tf_op jit(solution)/shard_map/all_to_all | solution.py:290
  98.1 7.6 %plane_next.3 = f32[32,8,128]{2,1,0:T(8,128)S(1)} custom-call(f32[32,8,128]{2,1,0:T(8,128)S(1)} %all_to_all.38.refs_0_, f32[3,96,128]{2,1,0:T(8,128)S(1)} %pad.4.refs_1_, bf16[256,256]{1,0:T(8,128)(2,1)S(1)} %copy-done, bf16[128,256]{1,0:T(8,128)(2,1)S(1)} %copy-done.7, bf16[192,192]{1,0:T(8,128)(2,1)S(1)} %copy-done.4, bf16[128,288]{1,0:T(8,128)(2,1)S(1)} %copy-done.3, ...), custom_call_target="tpu_custom_call" | custom-call | tf_op jit(solution)/shard_map/plane_next/pallas_call | solution.py:286
  105.7 13.9 %all_to_all.39.refs_0_ = f32[32,8,128]{2,1,0:T(8,128)S(1)} all-to-all(f32[32,8,128]{2,1,0:T(8,128)S(1)} %plane_next.3), channel_id=1, replica_groups=mesh['y'=4,'core'=2,'x'=4,'z'=8] {'x','z'}, dimensions={0} | all-to-all | bytes 262144 | tf_op jit(solution)/shard_map/all_to_all | solution.py:290
  119.6 1.4 stick_3.1
  121.0 13.8 %all_to_all.40.refs_0_ = f32[32,8,128]{2,1,0:T(8,128)S(1)} all-to-all(f32[32,8,128]{2,1,0:T(8,128)S(1)} %get-tuple-element.26), channel_id=1, replica_groups=mesh['y'=4,'core'=2,'x'=4,'z'=8] {'x','z'}, dimensions={0} | all-to-all | bytes 262144 | tf_op jit(solution)/shard_map/all_to_all | solution.py:290
  134.9 4.9 %plane_last.1 = f32[3,96,128]{2,1,0:T(8,128)S(1)} custom-call(f32[32,8,128]{2,1,0:T(8,128)S(1)} %all_to_all.40.refs_0_, f32[3,96,128]{2,1,0:T(8,128)S(1)} %get-tuple-element.27.refs_1_, bf16[256,256]{1,0:T(8,128)(2,1)S(1)} %copy-done, bf16[128,256]{1,0:T(8,128)(2,1)S(1)} %copy-done.7, bf16[192,192]{1,0:T(8,128)(2,1)S(1)} %copy-done.4, ...), custom_call_target="tpu_custom_call" | custom-call | tf_op jit(solution)/shard_map/plane_last/pallas_call | solution.py:286
  139.8 0.1 collective-permute-start
  139.9 1.4 collective-permute-done
  141.3 1.7 %collective-permute-start.1 = (f32[3,96,128]{2,1,0:T(8,128)S(1)}, f32[3,96,128]{2,1,0:T(8,128)S(1)}, u32[]{:S(2)}, u32[]{:S(2)}) collective-permute-start(f32[3,96,128]{2,1,0:T(8,128)S(1)} %add.17), channel_id=1, source_target_pairs={{0,64},{64,0},{128,192},{192,128},{1,65},{65,1},{129,193},{193,129... | collective-permute-start | bytes 442376 | tf_op jit(solution)/shard_map/ppermute | solution.py:295
  142.9 4.3 %collective-permute-done.1 = f32[3,96,128]{2,1,0:T(8,128)S(1)} collective-permute-done((f32[3,96,128]{2,1,0:T(8,128)S(1)}, f32[3,96,128]{2,1,0:T(8,128)S(1)}, u32[]{:S(2)}, u32[]{:S(2)}) %collective-permute-start.1) | collective-permute-done | bytes 147488 | tf_op jit(solution)/shard_map/ppermute | solution.py:295
  147.3 3.3 %collective-permute-start.2 = (f32[3,96,128]{2,1,0:T(8,128)S(1)}, f32[3,96,128]{2,1,0:T(8,128)S(1)}, u32[]{:S(2)}, u32[]{:S(2)}) collective-permute-start(f32[3,96,128]{2,1,0:T(8,128)S(1)} %add.18), channel_id=1, source_target_pairs={{0,128},{64,192},{128,0},{192,64},{1,129},{65,193},{129,1},{193,65... | collective-permute-start | bytes 442376 | tf_op jit(solution)/shard_map/ppermute | solution.py:295
  150.6 3.5 %collective-permute-done.2 = f32[3,96,128]{2,1,0:T(8,128)S(1)} collective-permute-done((f32[3,96,128]{2,1,0:T(8,128)S(1)}, f32[3,96,128]{2,1,0:T(8,128)S(1)}, u32[]{:S(2)}, u32[]{:S(2)}) %collective-permute-start.2) | collective-permute-done | bytes 147488 | tf_op jit(solution)/shard_map/ppermute | solution.py:295
  154.1 0.8 reshape.27
  (4 shorter events, 0.1 us)
Async XLA Ops:
  1.3 0.9 copy-start.1
  2.2 0.8 copy-start.8
  3.0 0.9 copy-start.11
  5.3 11.8 %copy-start.12 = (f32[3,9216]{1,0:T(4,128)S(1)}, f32[3,9216]{1,0:T(4,128)}, u32[]{:S(2)}) copy-start(f32[3,9216]{1,0:T(4,128)} %param.14) | copy-start | bytes 331780
  5.3 20.9 %all-to-all-start = ((f32[32,8,128]{2,1,0:T(8,128)}), f32[32,8,128]{2,1,0:T(8,128)S(1)}, u32[]{:S(2)}, u32[]{:S(2)}) async-start(f32[32,8,128]{2,1,0:T(8,128)} %get-tuple-element.15), calls=%async_computation | async-start | bytes 262144 | tf_op jit(solution)/shard_map/all_to_all | solution.py:290
  17.1 9.1 %copy-start.4 = (bf16[192,192]{1,0:T(8,128)(2,1)S(1)}, bf16[192,192]{1,0:T(8,128)(2,1)}, u32[]{:S(2)}) copy-start(bf16[192,192]{1,0:T(8,128)(2,1)} %constant.30.clone.refs_4_) | copy-start | bytes 221188
  17.1 9.1 %copy-start.6 = (bf16[256,128]{1,0:T(8,128)(2,1)S(1)}, bf16[256,128]{1,0:T(8,128)(2,1)}, u32[]{:S(2)}) copy-start(bf16[256,128]{1,0:T(8,128)(2,1)} %constant.32.clone.refs_6_) | copy-start | bytes 196612
  17.1 9.1 %copy-start.7 = (bf16[128,256]{1,0:T(8,128)(2,1)S(1)}, bf16[128,256]{1,0:T(8,128)(2,1)}, u32[]{:S(2)}) copy-start(bf16[128,256]{1,0:T(8,128)(2,1)} %constant.29.clone.refs_3_) | copy-start | bytes 196612
  17.3 8.9 %copy-start = (bf16[256,256]{1,0:T(8,128)(2,1)S(1)}, bf16[256,256]{1,0:T(8,128)(2,1)}, u32[]{:S(2)}) copy-start(bf16[256,256]{1,0:T(8,128)(2,1)} %constant.28.clone.refs_2_) | copy-start | bytes 393220
  17.3 8.9 %copy-start.3 = (bf16[128,288]{1,0:T(8,128)(2,1)S(1)}, bf16[128,288]{1,0:T(8,128)(2,1)}, u32[]{:S(2)}) copy-start(bf16[128,288]{1,0:T(8,128)(2,1)} %constant.31.clone.refs_5_) | copy-start | bytes 221188
  17.3 8.9 %copy-start.5 = (bf16[256,128]{1,0:T(8,128)(2,1)S(1)}, bf16[256,128]{1,0:T(8,128)(2,1)}, u32[]{:S(2)}) copy-start(bf16[256,128]{1,0:T(8,128)(2,1)} %constant.33.clone.refs_7_) | copy-start | bytes 196612
  33.8 14.1 %copy-start.2 = (bf16[256,256]{1,0:T(8,128)(2,1)S(1)}, bf16[256,256]{1,0:T(8,128)(2,1)}, u32[]{:S(2)}) copy-start(bf16[256,256]{1,0:T(8,128)(2,1)} %constant.25.clone.pair_ref.refs_6_) | copy-start | bytes 393220
  33.8 14.1 %copy-start.9 = (bf16[256,128]{1,0:T(8,128)(2,1)S(1)}, bf16[256,128]{1,0:T(8,128)(2,1)}, u32[]{:S(2)}) copy-start(bf16[256,128]{1,0:T(8,128)(2,1)} %constant.26.clone.low_ref.refs_7_) | copy-start | bytes 196612
  33.8 14.1 %copy-start.10 = (bf16[256,128]{1,0:T(8,128)(2,1)S(1)}, bf16[256,128]{1,0:T(8,128)(2,1)}, u32[]{:S(2)}) copy-start(bf16[256,128]{1,0:T(8,128)(2,1)} %constant.27.clone.refs_8_) | copy-start | bytes 196612
  139.8 1.5 collective-permute-start
  141.3 6.0 %collective-permute-start.1 = (f32[3,96,128]{2,1,0:T(8,128)S(1)}, f32[3,96,128]{2,1,0:T(8,128)S(1)}, u32[]{:S(2)}, u32[]{:S(2)}) collective-permute-start(f32[3,96,128]{2,1,0:T(8,128)S(1)} %add.17), channel_id=1, source_target_pairs={{0,64},{64,0},{128,192},{192,128},{1,65},{65,1},{129,193},{193,129... | collective-permute-start | bytes 442376 | tf_op jit(solution)/shard_map/ppermute | solution.py:295
  147.3 6.7 %collective-permute-start.2 = (f32[3,96,128]{2,1,0:T(8,128)S(1)}, f32[3,96,128]{2,1,0:T(8,128)S(1)}, u32[]{:S(2)}, u32[]{:S(2)}) collective-permute-start(f32[3,96,128]{2,1,0:T(8,128)S(1)} %add.18), channel_id=1, source_target_pairs={{0,128},{64,192},{128,0},{192,64},{1,129},{65,193},{129,1},{193,65... | collective-permute-start | bytes 442376 | tf_op jit(solution)/shard_map/ppermute | solution.py:295
